TPU v7x, 256 devices: a whole 4x4x8 slice. The times are simulated.
256 devices in a mesh: rve: 32 (over z, x), mic: 4 (over y), mac: 2 (over core).
Axes of the slice: x: 4, y: 4, z: 8, core: 2. Of those that a mesh axis runs over, the one named last changes fastest.
Arguments:
- displacement: float32 [3, 32, 8, 8], P(None, 'rve', ('mic', 'mac')), may hold values from -3 to 3
- plastic: float32 [2048, 6, 16, 256], P(('rve', 'mic', 'mac')), may hold values from -0.3 to 0.3
- bulk_modulus: float32 [16, 256], replicated, may hold values from 1 to 3
- shear_modulus: float32 [16, 256], replicated, may hold values from 0.5 to 1.5
- yield_radius: float32 [16, 256], replicated, may hold values from 0.05 to 0.3
- counts: int32 [2048], P(('rve', 'mic', 'mac')), may hold values from 0 to 3
- migration_plan: int32 [2048], P(('rve', 'mic', 'mac')), may hold values from 0 to 2047, as said below
Outputs:
- nodal_force: float32 [3, 32, 8, 8], P(None, 'rve', ('mic', 'mac'))
- plastic_new: float32 [2048, 6, 16, 256], P(('rve', 'mic', 'mac'))
Inputs may be any that keep to these rules, and one draw needn't show every extreme that they name: migration_plan is a permutation of 0 .. 2047. It keeps an RVE within the devices that share its mic and mac index; each device sends exactly 2 of its RVEs to each of 4 devices along rve and none to the others, so that every device receives 8. At each receiving device the RVEs are placed in order of rising iteration count.
All inputs are finite; a program needn't handle non-finite values.
Results may differ from a plain program's by a relative error of at most 0.0003.
Values sent between devices are 32-bit elements; how exact they have to be, the bound alone decides.
A program may use at most 128 MiB of HBM per device.

v0:
```python
import jax
import jax.numpy as jnp
from jax import lax
from jax.sharding import Mesh
from jax.sharding import PartitionSpec as P

RBLK = 4
RVE = ("rve_0", "rve_1")
RVE_MIC_MAC = ("rve_0", "rve_1", "mic", "mac")


REF_COUPLING = 0.7


def shifted(value, axis, steps):
    count = lax.axis_size(axis)
    first, last = (max(0, -steps), min(count, count - steps))
    return lax.ppermute(value, axis, [(source, source + steps) for source in range(first, last)])


def cut_along(array, dim, devices):
    shape = array.shape
    tiles = array.reshape(*shape[:dim], devices, shape[dim] // devices, *shape[dim + 1 :])
    return jnp.moveaxis(tiles, dim, 0)


def joined_along(tiles, dim):
    tiles = jnp.moveaxis(tiles, 0, dim)
    shape = tiles.shape
    return tiles.reshape(*shape[:dim], shape[dim] * shape[dim + 1], *shape[dim + 2 :])


def turned_blocks(tiles, axes, turns):
    shape = [lax.axis_size(a) for a in axes]
    tiles = tiles.reshape(*shape, *tiles.shape[1:])
    for k in turns:
        tiles = lax.all_to_all(tiles, axes[k], split_axis=k, concat_axis=k, tiled=True)
    return tiles.reshape(-1, *tiles.shape[len(axes) :])


def stepwise_exchange(array, axes, turns, split_dim, concat_dim):
    tiles = cut_along(array, split_dim, lax.axis_size(axes))
    return joined_along(turned_blocks(tiles, axes, turns), concat_dim)


def material_response(strain, plastic, bulk_modulus, shear_modulus, yield_radius):
    elastic = strain - plastic
    volumetric = elastic[..., 0, :, :, :] + elastic[..., 1, :, :, :] + elastic[..., 2, :, :, :]
    mean_normal = volumetric / 3.0
    deviator = jnp.stack(
        [
            elastic[..., 0, :, :, :] - mean_normal,
            elastic[..., 1, :, :, :] - mean_normal,
            elastic[..., 2, :, :, :] - mean_normal,
            elastic[..., 3, :, :, :],
            elastic[..., 4, :, :, :],
            elastic[..., 5, :, :, :],
        ],
        axis=-4,
    )
    trial_deviator = 2.0 * shear_modulus * deviator
    weights = jnp.array([1.0, 1.0, 1.0, 2.0, 2.0, 2.0], jnp.float32).reshape(6, 1, 1, 1)
    squared = jnp.sum(weights * trial_deviator * trial_deviator, axis=-4)
    factor = yield_radius / jnp.sqrt(jnp.maximum(squared, yield_radius * yield_radius))
    relaxed = factor[..., None, :, :, :] * trial_deviator
    normal_mask = jnp.array([1.0, 1.0, 1.0, 0.0, 0.0, 0.0], jnp.float32).reshape(6, 1, 1, 1)
    stress = relaxed + normal_mask * (bulk_modulus * volumetric)[..., None, :, :, :]
    increment = (trial_deviator - relaxed) / (2.0 * shear_modulus)
    return (stress, increment)


def green_apply(real_part, imag_part):
    extent = real_part.shape[-1]
    wavenumber = ((jnp.arange(extent) + extent // 2) % extent - extent // 2).astype(jnp.float32)
    freq_a = wavenumber[:, None, None]
    freq_b = wavenumber[None, :, None]
    freq_c = wavenumber[None, None, :]
    magnitude = freq_a * freq_a + freq_b * freq_b + freq_c * freq_c
    nonzero = magnitude > 0.0
    guarded = jnp.maximum(magnitude, 1.0)
    linear_term = jnp.where(nonzero, 1.0 / (2.0 * guarded), 0.0)
    cubic_term = jnp.where(nonzero, REF_COUPLING / (guarded * guarded), 0.0)

    def single(tau):
        tau_aa, tau_bb, tau_cc = (tau[:, 0], tau[:, 1], tau[:, 2])
        tau_bc, tau_ac, tau_ab = (tau[:, 3], tau[:, 4], tau[:, 5])
        traction_a = tau_aa * freq_a + tau_ab * freq_b + tau_ac * freq_c
        traction_b = tau_ab * freq_a + tau_bb * freq_b + tau_bc * freq_c
        traction_c = tau_ac * freq_a + tau_bc * freq_b + tau_cc * freq_c
        normal_part = freq_a * traction_a + freq_b * traction_b + freq_c * traction_c
        result_list = [
            linear_term * 2.0 * freq_a * traction_a - cubic_term * freq_a * freq_a * normal_part,
            linear_term * 2.0 * freq_b * traction_b - cubic_term * freq_b * freq_b * normal_part,
            linear_term * 2.0 * freq_c * traction_c - cubic_term * freq_c * freq_c * normal_part,
            linear_term * (freq_b * traction_c + freq_c * traction_b)
            - cubic_term * freq_b * freq_c * normal_part,
            linear_term * (freq_a * traction_c + freq_c * traction_a)
            - cubic_term * freq_a * freq_c * normal_part,
            linear_term * (freq_a * traction_b + freq_b * traction_a)
            - cubic_term * freq_a * freq_b * normal_part,
        ]
        return jnp.stack(result_list, axis=1)

    return (single(real_part), single(imag_part))


def transform_tables(extent):
    indices = jnp.arange(extent)
    angle = (
        2.0 * jnp.pi / extent * (indices[:, None] * indices[None, :] % extent).astype(jnp.float32)
    )
    plane = jnp.arange(extent * extent)
    row_b = plane // extent
    row_c = plane % extent
    phase = (row_b[:, None] * row_b[None, :] + row_c[:, None] * row_c[None, :]) % extent
    plane_angle = 2.0 * jnp.pi / extent * phase.astype(jnp.float32)
    return (jnp.cos(angle), jnp.sin(angle), jnp.cos(plane_angle), jnp.sin(plane_angle))


def polarization_update(stress, tables):
    cosine, sine, plane_cosine, plane_sine = tables
    highest = lax.Precision.HIGHEST
    batch = stress.shape[0]
    extent = stress.shape[-1]
    flat = stress.reshape(batch, 6, extent, extent * extent)
    real_part = jnp.einsum("bvxp,pq->bvxq", flat, plane_cosine, precision=highest)
    imag_part = -jnp.einsum("bvxp,pq->bvxq", flat, plane_sine, precision=highest)
    real_next = jnp.einsum("xk,bvxq->bvkq", cosine, real_part, precision=highest) + jnp.einsum(
        "xk,bvxq->bvkq", sine, imag_part, precision=highest
    )
    imag_next = jnp.einsum("xk,bvxq->bvkq", cosine, imag_part, precision=highest) - jnp.einsum(
        "xk,bvxq->bvkq", sine, real_part, precision=highest
    )
    shape_grid = (batch, 6, extent, extent, extent)
    real_part, imag_part = green_apply(real_next.reshape(shape_grid), imag_next.reshape(shape_grid))
    real_part = real_part.reshape(flat.shape)
    imag_part = imag_part.reshape(flat.shape)
    real_next = jnp.einsum("xk,bvxq->bvkq", cosine, real_part, precision=highest) - jnp.einsum(
        "xk,bvxq->bvkq", sine, imag_part, precision=highest
    )
    imag_next = jnp.einsum("xk,bvxq->bvkq", cosine, imag_part, precision=highest) + jnp.einsum(
        "xk,bvxq->bvkq", sine, real_part, precision=highest
    )
    spatial = jnp.einsum("bvxp,pq->bvxq", real_next, plane_cosine, precision=highest) - jnp.einsum(
        "bvxp,pq->bvxq", imag_next, plane_sine, precision=highest
    )
    return (spatial / float(extent**3)).reshape(shape_grid)


def solve_rows(plastic, strain_rows, counts, bulk_modulus, shear_modulus, yield_radius):
    width_rows = plastic.shape[0]
    extent = plastic.shape[2]
    bulk_grid = bulk_modulus.reshape(extent, extent, extent)
    shear_grid = shear_modulus.reshape(extent, extent, extent)
    radius_grid = yield_radius.reshape(extent, extent, extent)
    tables = transform_tables(extent)
    plastic_blocks = plastic.reshape(width_rows // RBLK, RBLK, 6, extent, extent, extent)
    strain_blocks = strain_rows.reshape(width_rows // RBLK, RBLK, 6)
    count_blocks = counts.reshape(width_rows // RBLK, RBLK)

    def solve_block(inputs):
        plastic_block, strain_block, count_block = inputs
        start = jnp.broadcast_to(strain_block[:, :, None, None, None], plastic_block.shape)
        highest_count = jnp.max(count_block)

        def sweep(step_index, carry):
            strain, previous_map, previous_update = carry
            stress, unused = material_response(
                strain, plastic_block, bulk_grid, shear_grid, radius_grid
            )
            update = polarization_update(stress, tables)
            mapped = strain - update
            change = update - previous_update
            numerator = jnp.mean(change * update, axis=(1, 2, 3, 4))
            denominator = jnp.mean(change * change, axis=(1, 2, 3, 4)) + 1e-06
            weight = jnp.where(step_index > 0, numerator / denominator, 0.0)
            candidate = mapped - weight[:, None, None, None, None] * (mapped - previous_map)
            active = step_index < count_block
            strain = jnp.where(active[:, None, None, None, None], candidate, strain)
            return (strain, mapped, update)

        final_strain, unused_map, unused_update = lax.fori_loop(
            0, highest_count, sweep, (start, start, jnp.zeros_like(start))
        )
        stress, increment = material_response(
            final_strain, plastic_block, bulk_grid, shear_grid, radius_grid
        )
        return (jnp.mean(stress, axis=(2, 3, 4)), plastic_block + increment)

    averages, updated = lax.map(solve_block, (plastic_blocks, strain_blocks, count_blocks))
    return (
        averages.reshape(width_rows, 6),
        updated.reshape(width_rows, 6, extent, extent * extent),
    )


def element_strain(displacement):
    rows_y = displacement.shape[2]
    depth = displacement.shape[3]
    upper_layer = shifted(displacement, RVE, -1)
    extended = jnp.concatenate([displacement, upper_layer], axis=1)
    upper_row = shifted(extended, ("mic", "mac"), -1)
    extended = jnp.concatenate([extended, upper_row], axis=2)
    extended = jnp.pad(extended, ((0, 0), (0, 0), (0, 0), (0, 1)))
    gradient = [[0.0, 0.0, 0.0], [0.0, 0.0, 0.0], [0.0, 0.0, 0.0]]
    for shift_a in (0, 1):
        for shift_b in (0, 1):
            for shift_c in (0, 1):
                corner_values = extended[
                    :, shift_a : shift_a + 1, shift_b : shift_b + rows_y, shift_c : shift_c + depth
                ]
                signs = ((2 * shift_a - 1) / 4.0, (2 * shift_b - 1) / 4.0, (2 * shift_c - 1) / 4.0)
                for component in range(3):
                    for direction in range(3):
                        gradient[component][direction] = (
                            gradient[component][direction]
                            + corner_values[component] * signs[direction]
                        )
    strain_field = jnp.stack(
        [
            gradient[0][0],
            gradient[1][1],
            gradient[2][2],
            0.5 * (gradient[1][2] + gradient[2][1]),
            0.5 * (gradient[0][2] + gradient[2][0]),
            0.5 * (gradient[0][1] + gradient[1][0]),
        ],
        axis=0,
    )
    return strain_field.reshape(6, rows_y * depth).T


def nodal_forces(averages, rows_y, depth):
    macro_stress = averages.T.reshape(6, 1, rows_y, depth)
    lower_layer = shifted(macro_stress, RVE, 1)
    extended = jnp.concatenate([lower_layer, macro_stress], axis=1)
    lower_row = shifted(extended, ("mic", "mac"), 1)
    extended = jnp.concatenate([lower_row, extended], axis=2)
    extended = jnp.pad(extended, ((0, 0), (0, 0), (0, 0), (1, 0)))
    pairs = [[0, 5, 4], [5, 1, 3], [4, 3, 2]]
    forces = [0.0, 0.0, 0.0]
    for shift_a in (0, 1):
        for shift_b in (0, 1):
            for shift_c in (0, 1):
                corner_values = extended[
                    :,
                    1 - shift_a : 2 - shift_a,
                    1 - shift_b : 1 - shift_b + rows_y,
                    1 - shift_c : 1 - shift_c + depth,
                ]
                signs = ((2 * shift_a - 1) / 4.0, (2 * shift_b - 1) / 4.0, (2 * shift_c - 1) / 4.0)
                for component in range(3):
                    for direction in range(3):
                        forces[component] = (
                            forces[component]
                            + corner_values[pairs[component][direction]] * signs[direction]
                        )
    return jnp.stack(forces, axis=0)


def route_slots(migration_plan, width_rows, capacity):
    columns = lax.axis_size("mic") * lax.axis_size("mac")
    target = migration_plan // width_rows
    partner = target // columns
    target_row = migration_plan % width_rows
    shared = partner[:, None] == partner[None, :]
    positions = jnp.arange(width_rows)
    earlier = positions[:, None] > positions[None, :]
    order_within = jnp.sum((shared & earlier).astype(jnp.int32), axis=1)
    return (partner * capacity + order_within, target_row)


def pack_rows(payload, slot_index, total_slots):
    matches = slot_index[None, :] == jnp.arange(total_slots)[:, None]
    source = jnp.sum(jnp.where(matches, jnp.arange(payload.shape[0])[None, :], 0), axis=1)
    filled = jnp.any(matches, axis=1)
    picked = jnp.take(payload, source, axis=0)
    return jnp.where(
        filled.reshape((-1,) + (1,) * (payload.ndim - 1)), picked, jnp.zeros_like(picked)
    )


def unpack_rows(received, labels, width_rows):
    wanted = labels.astype(jnp.int32) - 1
    matches = wanted[None, :] == jnp.arange(width_rows)[:, None]
    source = jnp.sum(jnp.where(matches, jnp.arange(received.shape[0])[None, :], 0), axis=1)
    return jnp.take(received, source, axis=0)


def on_device(
    displacement, plastic, bulk_modulus, shear_modulus, yield_radius, counts, migration_plan
):
    width_rows = plastic.shape[0]
    strain_rows = element_strain(displacement)
    devices_along = lax.axis_size(RVE)
    peers_used = min(devices_along // 2, width_rows // 2)
    capacity = width_rows // peers_used
    total_slots = devices_along * capacity
    slot_index, target_row = route_slots(migration_plan, width_rows, capacity)
    labels = (target_row + 1).astype(jnp.float32)
    extras = jnp.concatenate(
        [strain_rows, counts.astype(jnp.float32)[:, None], labels[:, None]], axis=1
    )
    outgoing = pack_rows(plastic, slot_index, total_slots)
    outgoing_extras = pack_rows(extras, slot_index, total_slots)
    arrived, arrived_extras = (
        lax.all_to_all(outgoing, RVE, split_axis=0, concat_axis=0, tiled=True),
        lax.all_to_all(outgoing_extras, RVE, split_axis=0, concat_axis=0, tiled=True),
    )
    arrived_labels = arrived_extras[:, 7]
    local_plastic = unpack_rows(arrived, arrived_labels, width_rows)
    local_extras = unpack_rows(arrived_extras, arrived_labels, width_rows)
    averages_here, plastic_new = solve_rows(
        local_plastic,
        local_extras[:, :6],
        local_extras[:, 6].astype(jnp.int32),
        bulk_modulus,
        shear_modulus,
        yield_radius,
    )
    filled = arrived_labels > 0.0
    positions = jnp.maximum(arrived_labels.astype(jnp.int32) - 1, 0)
    replies = jnp.where(filled[:, None], jnp.take(averages_here, positions, axis=0), 0.0)
    returned = stepwise_exchange(replies, RVE, (0, 1), 0, 0)
    averages = jnp.take(returned, slot_index, axis=0)
    force = nodal_forces(averages, displacement.shape[2], displacement.shape[3])
    return (force, plastic_new)


def solution(mesh):
    finer = Mesh(
        mesh.devices.reshape(8, 4, mesh.shape["mic"], mesh.shape["mac"]),
        ("rve_0", "rve_1", "mic", "mac"),
    )
    placed = (
        P(None, RVE, ("mic", "mac"), None),
        P(RVE_MIC_MAC, None, None, None),
        P(),
        P(),
        P(),
        P(RVE_MIC_MAC),
        P(RVE_MIC_MAC),
    )
    return jax.shard_map(
        on_device,
        mesh=finer,
        in_specs=placed,
        out_specs=(P(None, RVE, ("mic", "mac"), None), P(RVE_MIC_MAC, None, None, None)),
        check_vma=False,
    )
```

profile of v0, /device:TPU:24, one launch (start us, length us, event | category | flops | bytes accessed | tf_op | source)
XLA Modules:
  0.0 704.0 jit_solution(8029179027510344441)
XLA Ops:
  8.9 3.5 gather_fusion.2
  14.4 13.2 %all-to-all-start = ((f32[32,2,8]{2,1,0:T(2,128)}), f32[32,2,8]{2,1,0:T(2,128)S(1)}, u32[]{:S(2)}, u32[]{:S(2)}) async-start(f32[32,2,8]{2,1,0:T(2,128)} %select_select_fusion.1), calls=%async_computation | async-start | bytes 65536 | tf_op jit(solution)/shard_map/all_to_all | solution.py:308
  27.6 6.9 select_select_fusion
  37.4 7.1 %all-to-all-start.1 = ((f32[64,6,16,256]{3,2,1,0:T(8,128)}), f32[64,6,16,256]{3,2,1,0:T(8,128)}, u32[]{:S(2)}, u32[]{:S(2)}) async-start(f32[64,6,16,256]{3,2,1,0:T(8,128)} %select_select_fusion), calls=%async_computation.1 | async-start | bytes 12582912 | tf_op jit(solution)/shard_map/all_to_all | solution.py:307
  51.8 130.7 %all-to-all-done.1 = f32[64,6,16,256]{3,2,1,0:T(8,128)} async-done(((f32[64,6,16,256]{3,2,1,0:T(8,128)}), f32[64,6,16,256]{3,2,1,0:T(8,128)}, u32[]{:S(2)}, u32[]{:S(2)}) %all-to-all-start.1) | async-done | bytes 6291488 | tf_op jit(solution)/shard_map/all_to_all | solution.py:307
  182.6 3.4 gather_fusion.3
  186.0 4.0 gather.35
  190.0 6.3 broadcast_select_fusion.1
  196.3 131.9 %while.56 = (s32[]{:T(128)}, f32[2,4,6]{2,1,0:T(4,128)}, f32[2,4,6,16,16,16]{5,4,3,2,1,0:T(8,128)}, f32[16,256]{1,0:T(8,128)}, f32[16,16,16]{2,1,0:T(8,128)S(1)}...) while((s32[]{:T(128)}, f32[2,4,6]{2,1,0:T(4,128)}, ...), condition=%wide.region_13.14_spmd.clone.clone.clone.clone, body=%wide.region_4.13_spmd.sunk.clone.clone.clone.clone.sunk | while | flops 1368260864 | bytes 61317836 | solution.py:190
  196.3 3.9 dynamic-slice_bitcast_fusion.5
  212.2 3.3 fusion.229
  222.0 4.8 fusion.231
  228.6 3.9 dynamic-slice_bitcast_fusion.5
  244.0 67.8 %while.57 = (s32[]{:T(128)}, f32[4,6,16,16,16]{4,3,2,1,0:T(8,128)}, f32[4,6,16,16,16]{4,3,2,1,0:T(8,128)}, f32[4,6,16,16,16]{4,3,2,1,0:T(8,128)}, s32[]{:T(128)}...) while((s32[]{:T(128)}, f32[4,6,16,16,16]{4,3,2,1,0:T(8,128)}, ...), condition=%wide.wide.region_10.10_spmd.clone.clone, body=%wide.wide.region_6.9_spmd.sunk.clone.clone.sunk | while | flops 1364714240 | bytes 42464504 | solution.py:182
  244.6 3.3 sub.569
  269.3 3.7 multiply_subtract_fusion.17
  302.8 6.7 subtract_select_fusion.3
  311.8 3.3 fusion.229
  321.6 4.9 fusion.231
  331.0 211.7 %all-to-all-start.2 = ((f32[8,4,2,6]{3,1,2,0:T(4,128)}), f32[8,4,2,6]{3,1,2,0:T(4,128)S(1)}, u32[]{:S(2)}, u32[]{:S(2)}) async-start(f32[8,4,2,6]{3,1,2,0:T(4,128)} %fusion.76), calls=%async_computation.2 | async-start | bytes 65536 | tf_op jit(solution)/shard_map/all_to_all | solution.py:37
  543.3 7.4 %all-to-all-done.2 = f32[8,4,2,6]{3,1,2,0:T(4,128)S(1)} async-done(((f32[8,4,2,6]{3,1,2,0:T(4,128)}), f32[8,4,2,6]{3,1,2,0:T(4,128)S(1)}, u32[]{:S(2)}, u32[]{:S(2)}) %all-to-all-start.2) | async-done | bytes 1568 | tf_op jit(solution)/shard_map/all_to_all | solution.py:37
  554.7 5.4 all-to-all-done.3
  564.0 5.7 reshape.1186
  569.7 132.8 %collective-permute-start.3 = (f32[6,2,1,8]{3,0,2,1:T(8,128)S(1)}, f32[6,2,1,8]{3,0,2,1:T(8,128)S(1)}, u32[]{:S(2)}, u32[]{:S(2)}) collective-permute-start(f32[6,2,1,8]{3,0,2,1:T(8,128)S(1)} %pad_maximum_fusion), channel_id=1, source_target_pairs={{0,1},{1,2},{2,3},{3,4},{4,5},{5,6},{6,7},{8,9},{9,10},{10,11},{11... | collective-permute-start | bytes 1160 | tf_op jit(solution)/shard_map/ppermute | solution.py:18
  (294 shorter events, 125.3 us)
Async XLA Ops:
  0.6 8.3 %copy-start = (f32[8,6,16,256]{3,2,1,0:T(8,128)S(1)}, f32[8,6,16,256]{3,2,1,0:T(8,128)}, u32[]{:S(2)}) copy-start(f32[8,6,16,256]{3,2,1,0:T(8,128)} %param.16) | copy-start | bytes 2359300
  1.4 5.5 collective-permute-start
  6.9 5.6 collective-permute-start.1
  14.4 23.0 %all-to-all-start = ((f32[32,2,8]{2,1,0:T(2,128)}), f32[32,2,8]{2,1,0:T(2,128)S(1)}, u32[]{:S(2)}, u32[]{:S(2)}) async-start(f32[32,2,8]{2,1,0:T(2,128)} %select_select_fusion.1), calls=%async_computation | async-start | bytes 65536 | tf_op jit(solution)/shard_map/all_to_all | solution.py:308
  34.5 11.0 %copy-start.41 = (f32[16,256]{1,0:T(8,128)S(1)}, f32[16,256]{1,0:T(8,128)}, u32[]{:S(2)}) copy-start(f32[16,256]{1,0:T(8,128)} %param.18) | copy-start | bytes 49156
  37.4 145.1 %all-to-all-start.1 = ((f32[64,6,16,256]{3,2,1,0:T(8,128)}), f32[64,6,16,256]{3,2,1,0:T(8,128)}, u32[]{:S(2)}, u32[]{:S(2)}) async-start(f32[64,6,16,256]{3,2,1,0:T(8,128)} %select_select_fusion), calls=%async_computation.1 | async-start | bytes 12582912 | tf_op jit(solution)/shard_map/all_to_all | solution.py:307
  190.0 6.3 copy-start.32
  190.0 6.3 copy-start.36
  196.3 13.1 %copy-start.30 = (f32[1,16,16,16]{3,2,1,0:T(8,128)}, f32[1,16,16,16]{3,2,1,0:T(8,128)S(1)}, u32[]{:S(2)}) copy-start(f32[1,16,16,16]{3,2,1,0:T(8,128)S(1)} %get-tuple-element.1621) | copy-start | bytes 49156 | tf_op jit(solution)/shard_map/while
  228.6 13.1 %copy-start.30 = (f32[1,16,16,16]{3,2,1,0:T(8,128)}, f32[1,16,16,16]{3,2,1,0:T(8,128)S(1)}, u32[]{:S(2)}) copy-start(f32[1,16,16,16]{3,2,1,0:T(8,128)S(1)} %get-tuple-element.1621) | copy-start | bytes 49156 | tf_op jit(solution)/shard_map/while
  244.6 7.2 %copy-start.34 = (f32[16,256]{1,0:T(8,128)}, f32[16,256]{1,0:T(8,128)S(1)}, u32[]{:S(2)}) copy-start(f32[16,256]{1,0:T(8,128)S(1)} %get-tuple-element.1566) | copy-start | bytes 49156 | tf_op jit(solution)/shard_map/while/body/eval_jaxpr/while
  250.9 5.7 copy-start.9
  251.5 5.3 copy-start.3
  251.5 6.0 copy-start.12
  251.8 5.8 copy-start.38
  252.7 5.9 copy-start.16
  275.3 12.7 %copy-start.8 = (f32[4,1,16,16,16]{4,3,2,1,0:T(8,128)S(1)}, f32[4,1,16,16,16]{4,3,2,1,0:T(8,128)}, u32[]{:S(2)}) copy-start(f32[4,1,16,16,16]{4,3,2,1,0:T(8,128)} %get-tuple-element.1506) | copy-start | bytes 196612 | tf_op jit(solution)/shard_map/while/body/eval_jaxpr/while
  282.6 13.7 %copy-start.7 = (f32[4,1,16,16,16]{4,3,2,1,0:T(8,128)S(1)}, f32[4,1,16,16,16]{4,3,2,1,0:T(8,128)}, u32[]{:S(2)}) copy-start(f32[4,1,16,16,16]{4,3,2,1,0:T(8,128)} %get-tuple-element.1500) | copy-start | bytes 196612 | tf_op jit(solution)/shard_map/while/body/eval_jaxpr/while
  321.5 4.9 copy-start.15
  331.0 219.7 %all-to-all-start.2 = ((f32[8,4,2,6]{3,1,2,0:T(4,128)}), f32[8,4,2,6]{3,1,2,0:T(4,128)S(1)}, u32[]{:S(2)}, u32[]{:S(2)}) async-start(f32[8,4,2,6]{3,1,2,0:T(4,128)} %fusion.76), calls=%async_computation.2 | async-start | bytes 65536 | tf_op jit(solution)/shard_map/all_to_all | solution.py:37
  551.4 8.6 %all-to-all-start.3 = ((f32[8,4,2,6]{0,2,3,1:T(2,128)}), f32[8,4,2,6]{0,2,3,1:T(2,128)S(1)}, u32[]{:S(2)}, u32[]{:S(2)}) async-start(f32[8,4,2,6]{0,2,3,1:T(2,128)} %copy.155), calls=%async_computation.3 | async-start | bytes 49152 | tf_op jit(solution)/shard_map/all_to_all | solution.py:37
  561.5 8.2 %collective-permute-start.2 = (f32[6,1,1,8]{3,0,2,1:T(8,128)S(1)}, f32[6,1,1,8]{3,0,2,1:T(8,128)S(1)}, u32[]{:S(2)}, u32[]{:S(2)}) collective-permute-start(f32[6,1,1,8]{3,0,2,1:T(8,128)S(1)} %bitcast.334), channel_id=1, source_target_pairs={{0,8},{8,16},{16,24},{24,32},{32,40},{40,48},{48,56},{56,64},{64,7... | collective-permute-start | bytes 584 | tf_op jit(solution)/shard_map/ppermute | solution.py:18
  564.0 140.1 %copy-start.1 = (f32[8,6,16,256]{3,2,1,0:T(8,128)S(1)}, f32[8,6,16,256]{3,2,1,0:T(8,128)}, u32[]{:S(2)}) copy-start(f32[8,6,16,256]{3,2,1,0:T(8,128)} %param.16) | copy-start | bytes 2359300
  569.7 133.6 %collective-permute-start.3 = (f32[6,2,1,8]{3,0,2,1:T(8,128)S(1)}, f32[6,2,1,8]{3,0,2,1:T(8,128)S(1)}, u32[]{:S(2)}, u32[]{:S(2)}) collective-permute-start(f32[6,2,1,8]{3,0,2,1:T(8,128)S(1)} %pad_maximum_fusion), channel_id=1, source_target_pairs={{0,1},{1,2},{2,3},{3,4},{4,5},{5,6},{6,7},{8,9},{9,10},{10,11},{11... | collective-permute-start | bytes 1160 | tf_op jit(solution)/shard_map/ppermute | solution.py:18
  (43 other events, 125.8 us)
where the time goes:
time: 705 us; the launch traced here: 704 us
  starting transfers between devices  374 us (53%)
  waiting for transfers between devices  148 us (21%)
  local copies, waits for them, and re-layouts  90.6 us (13%)
  other arithmetic  79.1 us (11%)
  matrix products  8.98 us (1%)
    all_to_all x2, starting transfers between devices, turned_blocks(): lax.all_to_all(tiles, axes[k], split_axis=k, concat_axis=k, tiled=True)  215 us
    ppermute x4, starting transfers between devices, shifted(): lax.ppermute(value, axis, [(source, source + steps) for source in range(f...  138 us
    all_to_all x1, waiting for transfers between devices, on_device(): lax.all_to_all(outgoing, RVE, split_axis=0, concat_axis=0, tiled=True)  131 us
  transfers between devices with their start and end apart: 8, of which 6 were waited for; matrix products, arithmetic and copies ran while one was open for 4% of the time, Pallas kernels for 0%

commit v1 on v0

v1 whole, which is shorter than its diff:
```python
import math

import jax
import jax.numpy as jnp
import numpy as np
from jax import lax
from jax.experimental import pallas as pl
from jax.experimental.pallas import tpu as pltpu
from jax.sharding import Mesh
from jax.sharding import PartitionSpec as P

RVE = ("rve_0", "rve_1")
RVE_MIC_MAC = ("rve_0", "rve_1", "mic", "mac")


COUPLING = 0.7
PAIRS = ((0, 0), (1, 1), (2, 2), (1, 2), (0, 2), (0, 1))


def transform_tables(n):
    plane = np.arange(n * n)
    b, c = plane // n, plane % n
    angle = 2.0 * np.pi / n * ((np.outer(b, b) + np.outer(c, c)) % n)
    table = np.concatenate([np.cos(angle), np.sin(angle)], axis=1).astype(np.float32)
    high = table.astype(jnp.bfloat16)
    low = (table - high.astype(np.float32)).astype(jnp.bfloat16)
    return np.concatenate([high, high, low], axis=0)


def green_table(n):
    index = np.stack(np.meshgrid(np.arange(n), np.arange(n), np.arange(n), indexing="ij"))

    def operator(i):
        k = ((i + n // 2) % n - n // 2).astype(np.float64)
        q = np.sum(k * k, axis=0)
        safe = np.maximum(q, 1.0)
        rows = []
        for m, r in PAIRS:
            row = []
            for p, s in PAIRS:
                eye = lambda u, v: 1.0 if u == v else 0.0
                first = (
                    eye(m, p) * k[r] * k[s] + eye(m, s) * k[r] * k[p] + eye(r, p) * k[m] * k[s] + eye(r, s) * k[m] * k[p]
                ) / (4.0 * safe)
                row.append(first - COUPLING * k[m] * k[r] * k[p] * k[s] / (safe * safe))
            rows.append(row)
        return np.where(q > 0, np.array(rows), 0.0)

    even = 0.5 * (operator(index) + operator((-index) % n)) / float(n**3)
    even = even[:, :, : n // 2 + 1]
    rows = [even[i, j].reshape(n // 2 + 1, n * n) for i in range(6) for j in range(i, 6)]
    table = np.stack(rows, axis=1).reshape(-1, n * n).astype(np.float32)
    return np.pad(table, ((0, -table.shape[0] % 8), (0, 0)))


def turn(k, n, value, sign):
    re, im = value
    if k == 0:
        return value
    if 4 * k == n:
        return (im, -re) if sign < 0 else (-im, re)
    if 8 * k == n:
        r = math.sqrt(0.5)
        return ((re + im) * r, (im - re) * r) if sign < 0 else ((re - im) * r, (re + im) * r)
    c, s = math.cos(2 * math.pi * k / n), sign * math.sin(2 * math.pi * k / n)
    return (re * c - im * s, re * s + im * c)


def real_forward(x):
    n = len(x)
    if n == 2:
        return [(x[0] + x[1], None), (x[0] - x[1], None)]
    even, odd = real_forward(x[0::2]), real_forward(x[1::2])
    out = [None] * (n // 2 + 1)
    out[0] = (even[0][0] + odd[0][0], None)
    out[n // 2] = (even[0][0] - odd[0][0], None)
    for k in range(1, n // 4 + 1):
        if 4 * k == n:
            out[k] = (even[k][0], -odd[k][0])
        else:
            t = turn(k, n, odd[k], -1)
            out[k] = (even[k][0] + t[0], even[k][1] + t[1])
            out[n // 2 - k] = (even[k][0] - t[0], t[1] - even[k][1])
    return out


def real_backward(y):
    n = 2 * (len(y) - 1)
    if n == 2:
        return [y[0][0] + y[1][0], y[0][0] - y[1][0]]
    even, odd = [None] * (n // 4 + 1), [None] * (n // 4 + 1)
    even[0] = (y[0][0] + y[n // 2][0], None)
    odd[0] = (y[0][0] - y[n // 2][0], None)
    for k in range(1, n // 4 + 1):
        if 4 * k == n:
            even[k] = (2.0 * y[k][0], None)
            odd[k] = (-2.0 * y[k][1], None)
        else:
            o = y[n // 2 - k]
            even[k] = (y[k][0] + o[0], y[k][1] - o[1])
            odd[k] = turn(k, n, (y[k][0] - o[0], y[k][1] + o[1]), 1)
    out = [None] * n
    out[0::2] = real_backward(even)
    out[1::2] = real_backward(odd)
    return out


def flow_rule(elastic, shear2, radius):
    volume = elastic[0] + elastic[1] + elastic[2]
    mean = volume * (1.0 / 3.0)
    deviator = [elastic[i] - mean for i in range(3)] + list(elastic[3:])
    trial = [shear2 * d for d in deviator]
    normal = trial[0] * trial[0] + trial[1] * trial[1] + trial[2] * trial[2]
    mixed = trial[3] * trial[3] + trial[4] * trial[4] + trial[5] * trial[5]
    squared = normal + (mixed + mixed)
    factor = radius * lax.rsqrt(jnp.maximum(squared, radius * radius))
    return volume, deviator, trial, factor


HALVES = (slice(0, 128), slice(128, 256))


def solve_kernel(
    plastic_ref, macro_ref, counts_ref, bulk_ref, shear_ref, radius_ref, dft_ref, green_ref,
    next_ref, mean_ref,
    halves_s, copy_sem, material_s, green_s, plastic_s, strain_s, stress_s, update_s, mapped_s, left_s, product_s, left2_s, product2_s,
):
    f32, bf16 = jnp.float32, jnp.bfloat16
    counts = counts_ref[...]
    incoming = [
        pltpu.make_async_copy(plastic_ref.at[:, lanes], halves_s.at[h], copy_sem.at[h]) for h, lanes in enumerate(HALVES)
    ]
    for copy in incoming:
        copy.start()
    for a in range(16):
        shear2 = 2.0 * shear_ref[a : a + 1, :]
        for i, row in enumerate((shear2, bulk_ref[a : a + 1, :], radius_ref[a : a + 1, :])):
            material_s[a, i] = jnp.broadcast_to(row, (8, 256))

    @pl.loop(0, 24)
    def _(block):
        rows = green_ref[pl.ds(pl.multiple_of(block * 8, 8), 8), :]
        for r in range(8):
            green_s[block * 8 + r] = jnp.broadcast_to(rows[r : r + 1, :], (8, 256))

    for copy in incoming:
        copy.wait()

    @pl.loop(0, 96, unroll=4)
    def _(row):
        for h, lanes in enumerate(HALVES):
            plastic_s[row, :, lanes] = halves_s[h, pl.ds(row, 8, stride=96), :]

    for c in range(6):
        start = jnp.broadcast_to(macro_ref[:, c : c + 1], (8, 256))

        @pl.loop(0, 16)
        def _(a):
            strain_s[c * 16 + a] = start

    def split(value):
        high = value.astype(bf16)
        low = (value - high.astype(f32)).astype(bf16)
        return high, low

    def polarization():
        @pl.loop(0, 16)
        def _(a):
            for lanes in HALVES:
                shear2 = material_s[a, 0, :, lanes]
                bulk = material_s[a, 1, :, lanes]
                radius = material_s[a, 2, :, lanes]
                elastic = [strain_s[c * 16 + a, :, lanes] - plastic_s[c * 16 + a, :, lanes] for c in range(6)]
                volume, _, trial, factor = flow_rule(elastic, shear2, radius)
                pressure = bulk * volume
                for c in range(6):
                    value = factor * trial[c]
                    stress_s[c * 16 + a, :, lanes] = value + pressure if c < 3 else value

        @pl.loop(0, 3)
        def _(pair):
            for lanes in HALVES:
                sets = []
                for half in range(2):
                    y = real_forward([stress_s[pair * 32 + half * 16 + a, :, lanes] for a in range(16)])
                    sets.append([y[0][0], y[8][0]] + [part for k in range(1, 8) for part in y[k]])
                rows = pl.ds(pl.multiple_of(pair * 16, 16), 16)
                for r in range(16):
                    high, low = split(jnp.concatenate([sets[0][r], sets[1][r]], axis=0))
                    left_s[r, rows, lanes] = high
                    left_s[r, rows, slice(256 + lanes.start, 256 + lanes.stop)] = low

        left = left_s[...].reshape(768, 512)
        product_s[...] = jnp.dot(
            jnp.concatenate([left, left[:, :256]], axis=1), dft_ref[...], preferred_element_type=f32
        ).reshape(16, 48, 512)

        def operate(k, re, im, lanes):
            for t, value in ((2 * k, re), (2 * k + 1, im)):
                value = value[:3] + [v + v for v in value[3:]]
                out = [None] * 6
                j = 0
                for i in range(6):
                    for m in range(i, 6):
                        g = green_s[k * 21 + j, :, lanes]
                        j += 1
                        out[i] = g * value[m] if out[i] is None else out[i] + g * value[m]
                        if m != i:
                            out[m] = g * value[i] if out[m] is None else out[m] + g * value[i]
                for pair in range(3):
                    high, low = split(jnp.concatenate([out[2 * pair], out[2 * pair + 1]], axis=0))
                    left2_s[t, slice(pair * 16, pair * 16 + 16), lanes] = high
                    left2_s[t, slice(pair * 16, pair * 16 + 16), slice(256 + lanes.start, 256 + lanes.stop)] = low

        for k, row in ((0, 0), (8, 1)):
            for lanes in HALVES:
                wide = slice(256 + lanes.start, 256 + lanes.stop)
                re = [product_s[row, slice(c * 8, c * 8 + 8), lanes] for c in range(6)]
                im = [-product_s[row, slice(c * 8, c * 8 + 8), wide] for c in range(6)]
                operate(k, re, im, lanes)

        @pl.loop(1, 8)
        def _(k):
            for lanes in HALVES:
                wide = slice(256 + lanes.start, 256 + lanes.stop)
                re, im = [], []
                for c in range(6):
                    rows = slice(c * 8, c * 8 + 8)
                    re.append(product_s[2 * k, rows, lanes] + product_s[2 * k + 1, rows, wide])
                    im.append(product_s[2 * k + 1, rows, lanes] - product_s[2 * k, rows, wide])
                operate(k, re, im, lanes)

        left2 = left2_s[...].reshape(864, 512)
        product2_s[...] = jnp.dot(
            jnp.concatenate([left2, left2[:, :256]], axis=1), dft_ref[...], preferred_element_type=f32
        ).reshape(18, 48, 512)

    def update_of(c, lanes):
        wide = slice(256 + lanes.start, 256 + lanes.stop)
        rows = pl.ds(pl.multiple_of(c * 8, 8), 8)
        y = []
        for k in range(9):
            re = product2_s[2 * k, rows, lanes] - product2_s[2 * k + 1, rows, wide]
            im = None if k in (0, 8) else product2_s[2 * k, rows, wide] + product2_s[2 * k + 1, rows, lanes]
            y.append((re, im))
        return real_backward(y)

    polarization()
    active = counts > 0

    @pl.loop(0, 6)
    def _(c):
        for lanes in HALVES:
            update = update_of(c, lanes)
            for a in range(16):
                strain = strain_s[c * 16 + a, :, lanes]
                strain_s[c * 16 + a, :, lanes] = jnp.where(active, strain - update[a], strain)
                update_s[c * 16 + a, :, lanes] = update[a]
                mapped_s[c * 16 + a, :, lanes] = strain - update[a]

    @pl.loop(1, 3)
    def _(step):
        polarization()
        zero = jnp.zeros((8, 128), f32)

        def gather(c, carry):
            numerator, denominator = carry
            for lanes in HALVES:
                update = update_of(c, lanes)
                for a in range(16):
                    change = update[a] - update_s[c * 16 + a, :, lanes]
                    numerator = numerator + change * update[a]
                    denominator = denominator + change * change
                    update_s[c * 16 + a, :, lanes] = update[a]
            return numerator, denominator

        numerator, denominator = lax.fori_loop(0, 6, gather, (zero, zero))
        scale = 1.0 / float(6 * 16**3)
        numerator = jnp.sum(numerator, axis=1, keepdims=True) * scale
        denominator = jnp.sum(denominator, axis=1, keepdims=True) * scale + 1e-06
        weight = jnp.broadcast_to(numerator / denominator, (8, 256))
        active = jnp.broadcast_to(step < counts, (8, 256))

        @pl.loop(0, 96, unroll=4)
        def _(row):
            strain = strain_s[row]
            mapped = strain - update_s[row]
            candidate = mapped - weight * (mapped - mapped_s[row])
            mapped_s[row] = mapped
            strain_s[row] = jnp.where(active, candidate, strain)

    def finish(a, sums):
        sums = list(sums)
        for lanes in HALVES:
            shear2 = material_s[a, 0, :, lanes]
            bulk = material_s[a, 1, :, lanes]
            radius = material_s[a, 2, :, lanes]
            plastic = [plastic_s[c * 16 + a, :, lanes] for c in range(6)]
            elastic = [strain_s[c * 16 + a, :, lanes] - plastic[c] for c in range(6)]
            volume, deviator, trial, factor = flow_rule(elastic, shear2, radius)
            pressure = bulk * volume
            for c in range(6):
                value = factor * trial[c]
                sums[c] = sums[c] + (value + pressure if c < 3 else value)
                plastic_s[c * 16 + a, :, lanes] = plastic[c] + (deviator[c] - factor * deviator[c])
        return tuple(sums)

    zero = jnp.zeros((8, 128), f32)
    sums = lax.fori_loop(0, 16, finish, (zero,) * 6)
    lane = lax.broadcasted_iota(jnp.int32, (8, 128), 1)
    means = zero
    for c in range(6):
        means = jnp.where(lane == c, jnp.sum(sums[c], axis=1, keepdims=True) * (1.0 / 4096.0), means)
    mean_ref[...] = means

    @pl.loop(0, 96, unroll=4)
    def _(row):
        for h, lanes in enumerate(HALVES):
            halves_s[h, pl.ds(row, 8, stride=96), :] = plastic_s[row, :, lanes]

    outgoing = [
        pltpu.make_async_copy(halves_s.at[h], next_ref.at[:, lanes], copy_sem.at[h]) for h, lanes in enumerate(HALVES)
    ]
    for copy in outgoing:
        copy.start()
    for copy in outgoing:
        copy.wait()


def solve(plastic, macro, counts, bulk, shear, radius):
    f32, bf16 = jnp.float32, jnp.bfloat16
    vm = pl.BlockSpec(memory_space=pltpu.VMEM)
    updated, means = pl.pallas_call(
        solve_kernel,
        out_shape=(jax.ShapeDtypeStruct((768, 256), f32), jax.ShapeDtypeStruct((8, 128), f32)),
        in_specs=[pl.BlockSpec(memory_space=pl.ANY)] + [vm] * 7,
        out_specs=(pl.BlockSpec(memory_space=pl.ANY), vm),
        scratch_shapes=[
            pltpu.VMEM((2, 768, 128), f32),
            pltpu.SemaphoreType.DMA((2,)),
            pltpu.VMEM((16, 3, 8, 256), f32),
            pltpu.VMEM((192, 8, 256), f32),
            pltpu.VMEM((96, 8, 256), f32),
            pltpu.VMEM((96, 8, 256), f32),
            pltpu.VMEM((96, 8, 256), f32),
            pltpu.VMEM((96, 8, 256), f32),
            pltpu.VMEM((96, 8, 256), f32),
            pltpu.VMEM((16, 48, 512), bf16),
            pltpu.VMEM((16, 48, 512), f32),
            pltpu.VMEM((18, 48, 512), bf16),
            pltpu.VMEM((18, 48, 512), f32),
        ],
        compiler_params=pltpu.CompilerParams(vmem_limit_bytes=48 << 20),
        name="solve",
    )(
        plastic.reshape(768, 256),
        macro,
        counts[:, None],
        bulk,
        shear,
        radius,
        jnp.asarray(transform_tables(16)),
        jnp.asarray(green_table(16)),
    )
    return updated, means


def shifted(value, axis, steps):
    count = lax.axis_size(axis)
    first, last = (max(0, -steps), min(count, count - steps))
    return lax.ppermute(value, axis, [(source, source + steps) for source in range(first, last)])


def element_strain(displacement):
    rows_y = displacement.shape[2]
    depth = displacement.shape[3]
    upper_layer = shifted(displacement, RVE, -1)
    extended = jnp.concatenate([displacement, upper_layer], axis=1)
    upper_row = shifted(extended, ("mic", "mac"), -1)
    extended = jnp.concatenate([extended, upper_row], axis=2)
    extended = jnp.pad(extended, ((0, 0), (0, 0), (0, 0), (0, 1)))
    gradient = [[0.0, 0.0, 0.0], [0.0, 0.0, 0.0], [0.0, 0.0, 0.0]]
    for shift_a in (0, 1):
        for shift_b in (0, 1):
            for shift_c in (0, 1):
                corner_values = extended[
                    :, shift_a : shift_a + 1, shift_b : shift_b + rows_y, shift_c : shift_c + depth
                ]
                signs = ((2 * shift_a - 1) / 4.0, (2 * shift_b - 1) / 4.0, (2 * shift_c - 1) / 4.0)
                for component in range(3):
                    for direction in range(3):
                        gradient[component][direction] = (
                            gradient[component][direction]
                            + corner_values[component] * signs[direction]
                        )
    strain_field = jnp.stack(
        [
            gradient[0][0],
            gradient[1][1],
            gradient[2][2],
            0.5 * (gradient[1][2] + gradient[2][1]),
            0.5 * (gradient[0][2] + gradient[2][0]),
            0.5 * (gradient[0][1] + gradient[1][0]),
        ],
        axis=0,
    )
    return strain_field.reshape(6, rows_y * depth).T


def nodal_forces(averages, rows_y, depth):
    macro_stress = averages.T.reshape(6, 1, rows_y, depth)
    lower_layer = shifted(macro_stress, RVE, 1)
    extended = jnp.concatenate([lower_layer, macro_stress], axis=1)
    lower_row = shifted(extended, ("mic", "mac"), 1)
    extended = jnp.concatenate([lower_row, extended], axis=2)
    extended = jnp.pad(extended, ((0, 0), (0, 0), (0, 0), (1, 0)))
    pairs = [[0, 5, 4], [5, 1, 3], [4, 3, 2]]
    forces = [0.0, 0.0, 0.0]
    for shift_a in (0, 1):
        for shift_b in (0, 1):
            for shift_c in (0, 1):
                corner_values = extended[
                    :,
                    1 - shift_a : 2 - shift_a,
                    1 - shift_b : 1 - shift_b + rows_y,
                    1 - shift_c : 1 - shift_c + depth,
                ]
                signs = ((2 * shift_a - 1) / 4.0, (2 * shift_b - 1) / 4.0, (2 * shift_c - 1) / 4.0)
                for component in range(3):
                    for direction in range(3):
                        forces[component] = (
                            forces[component]
                            + corner_values[pairs[component][direction]] * signs[direction]
                        )
    return jnp.stack(forces, axis=0)


def route_slots(migration_plan, width_rows, capacity):
    columns = lax.axis_size("mic") * lax.axis_size("mac")
    target = migration_plan // width_rows
    partner = target // columns
    target_row = migration_plan % width_rows
    shared = partner[:, None] == partner[None, :]
    positions = jnp.arange(width_rows)
    earlier = positions[:, None] > positions[None, :]
    order_within = jnp.sum((shared & earlier).astype(jnp.int32), axis=1)
    return (partner * capacity + order_within, target_row)


def pack_rows(payload, slot_index, total_slots):
    matches = slot_index[None, :] == jnp.arange(total_slots)[:, None]
    source = jnp.sum(jnp.where(matches, jnp.arange(payload.shape[0])[None, :], 0), axis=1)
    filled = jnp.any(matches, axis=1)
    picked = jnp.take(payload, source, axis=0)
    return jnp.where(
        filled.reshape((-1,) + (1,) * (payload.ndim - 1)), picked, jnp.zeros_like(picked)
    )


def unpack_rows(received, labels, width_rows):
    wanted = labels.astype(jnp.int32) - 1
    matches = wanted[None, :] == jnp.arange(width_rows)[:, None]
    source = jnp.sum(jnp.where(matches, jnp.arange(received.shape[0])[None, :], 0), axis=1)
    return jnp.take(received, source, axis=0)


def on_device(
    displacement, plastic, bulk_modulus, shear_modulus, yield_radius, counts, migration_plan
):
    width_rows, depth = plastic.shape[0], displacement.shape[3]
    strain_rows = element_strain(displacement)
    updated, means = solve(
        plastic, strain_rows, counts, bulk_modulus, shear_modulus, yield_radius
    )
    devices_along = lax.axis_size(RVE)
    capacity = 2
    total_slots = devices_along * capacity
    slot_index, target_row = route_slots(migration_plan, width_rows, capacity)
    labels = (target_row + 1)[:, None]
    outgoing = pack_rows(updated.reshape(plastic.shape), slot_index, total_slots)
    outgoing_labels = pack_rows(labels, slot_index, total_slots)
    arrived = lax.all_to_all(outgoing, RVE, split_axis=0, concat_axis=0, tiled=True)
    arrived_labels = lax.all_to_all(
        outgoing_labels, RVE, split_axis=0, concat_axis=0, tiled=True
    )
    plastic_new = unpack_rows(arrived, arrived_labels[:, 0], width_rows)
    force = nodal_forces(means[:, :6], displacement.shape[2], depth)
    return (force, plastic_new)


def solution(mesh):
    finer = Mesh(
        mesh.devices.reshape(8, 4, mesh.shape["mic"], mesh.shape["mac"]),
        ("rve_0", "rve_1", "mic", "mac"),
    )
    placed = (
        P(None, RVE, ("mic", "mac"), None),
        P(RVE_MIC_MAC, None, None, None),
        P(),
        P(),
        P(),
        P(RVE_MIC_MAC),
        P(RVE_MIC_MAC),
    )
    return jax.shard_map(
        on_device,
        mesh=finer,
        in_specs=placed,
        out_specs=(P(None, RVE, ("mic", "mac"), None), P(RVE_MIC_MAC, None, None, None)),
        check_vma=False,
    )
```

time: 705 us -> 232 us (0.33)
  the two profiles are of different devices: /device:TPU:24 before, /device:TPU:119 now
where the time goes in v1:
time: 232 us; the launch traced here: 231 us
  waiting for transfers between devices  146 us (63%)
  starting transfers between devices  30.4 us (13%)
  Pallas kernels  19.2 us (8%)
  other arithmetic  19.1 us (8%)
  local copies, waits for them, and re-layouts  15.6 us (7%)
    ppermute x4, waiting for transfers between devices, shifted(): lax.ppermute(value, axis, [(source, source + steps) for source in range(f...  126 us
    all_to_all x1, waiting for transfers between devices, on_device(): lax.all_to_all(outgoing, RVE, split_axis=0, concat_axis=0, tiled=True)  20.4 us
    pallas_call x1, Pallas kernels, solve(): pl.pallas_call(solve_kernel, out_shape=(jax.ShapeDtypeStruct((768, 256),...  19.2 us
    ppermute x4, starting transfers between devices, shifted(): lax.ppermute(value, axis, [(source, source + steps) for source in range(f...  12.1 us
    all_to_all x1, starting transfers between devices, on_device(): lax.all_to_all(outgoing_labels, RVE, split_axis=0, concat_axis=0, tiled=T...  9.37 us
    all_to_all x1, starting transfers between devices, on_device(): lax.all_to_all(outgoing, RVE, split_axis=0, concat_axis=0, tiled=True)  8.97 us
    select_n x2, other arithmetic, pack_rows(): jnp.where(filled.reshape((-1,) + (1,) * (payload.ndim - 1)), picked, jnp....  7.58 us
    unnamed x14, local copies, waits for them, and re-layouts  6.59 us
  transfers between devices with their start and end apart: 6, of which 4 were waited for; matrix products, arithmetic and copies ran while one was open for 10% of the time, Pallas kernels for 8%

profile of v1, /device:TPU:119, one launch (start us, length us, event | category | flops | bytes accessed | tf_op | source)
XLA Modules:
  0.0 231.4 jit_solution(15820402537020443877)
XLA Ops:
  1.3 2.4 %collective-permute-start = (f32[3,1,1,8]{3,0,2,1:T(4,128)S(1)}, f32[3,1,1,8]{3,0,2,1:T(4,128)S(1)}, u32[]{:S(2)}, u32[]{:S(2)}) collective-permute-start(f32[3,1,1,8]{3,0,2,1:T(4,128)S(1)} %get-tuple-element.19), channel_id=1, source_target_pairs={{8,0},{16,8},{24,16},{32,24},{40,32},{48,40},{56,48},{64,56},{72,6... | collective-permute-start | bytes 296 | tf_op jit(solution)/shard_map/ppermute | solution.py:371
  5.7 5.0 %compare_select_fusion.5 = s32[64]{0:T(128)S(1)} fusion(s32[]{:T(128)} %bitcast.14, s32[]{:T(128)} %bitcast.15, s32[]{:T(128)} %bitcast.16, s32[]{:T(128)} %bitcast.17, s32[]{:T(128)} %bitcast.18, s32[]{:T(128)} %bitcast.19, s32[]{:T(128)} %bitcast.20, s32[]{:T(128)} %bitcast.21, s32[64]{0:T(128)S(1)} %select_reduce_fusion.1), kind=kLoop, calls=%fused_computation.39 | loop fusion | flops 1088 | bytes 544 | tf_op jit(solution)/shard_map/jit(_take)/gather | solution.py:454
  11.5 9.4 %all-to-all-start = ((s32[32,2,1]{1,2,0:T(1,128)}), s32[32,2,1]{1,2,0:T(1,128)S(1)}, u32[]{:S(2)}, u32[]{:S(2)}) async-start(s32[32,2,1]{1,2,0:T(1,128)} %bitcast.22), calls=%async_computation | async-start | bytes 32768 | tf_op jit(solution)/shard_map/all_to_all | solution.py:483
  20.9 3.4 %collective-permute-start.1 = (f32[3,2,1,8]{3,0,2,1:T(4,128)S(1)}, f32[3,2,1,8]{3,0,2,1:T(4,128)S(1)}, u32[]{:S(2)}, u32[]{:S(2)}) collective-permute-start(f32[3,2,1,8]{3,0,2,1:T(4,128)S(1)} %constant_dynamic-update-slice_fusion), channel_id=1, source_target_pairs={{1,0},{2,1},{3,2},{4,3},{5,4},{6,5},{7,6},{9,8},{10,9},{11,10},{12... | collective-permute-start | bytes 584 | tf_op jit(solution)/shard_map/ppermute | solution.py:371
  25.1 1.7 collective-permute-done.1
  26.8 0.7 add_add_fusion.2
  27.6 0.8 add_add_fusion
  28.3 0.8 add_multiply_fusion.2
  29.1 0.8 add_multiply_fusion.1
  29.8 0.8 add_multiply_fusion
  30.7 1.1 copy-done
  31.8 1.1 copy-done.1
  33.0 0.9 copy-done.2
  36.0 19.2 %solve.1 = (f32[768,256]{1,0:T(8,128)S(1)}, f32[8,128]{1,0:T(8,128)S(1)}) custom-call(f32[768,256]{1,0:T(8,128)S(1)} %bitcast.88, f32[8,6]{1,0:T(8,128)S(1)} %bitcast.89, s32[8,1]{1,0:T(8,128)S(1)} %copy.54.counts_ref, f32[16,256]{1,0:T(8,128)S(1)} %copy-done.3, f32[16,256]{1,0:T(8,128)S(1)} %copy-done.4, f32[16,256]{1,0:T(8,128)S(1)} %copy-done.5, ...), custom_call_target="tpu_custom_call" | custom-call | tf_op jit(solution)/shard_map/solve/pallas_call | solution.py:333
  55.2 3.6 %gather_fusion = f32[64,6,16,256]{3,2,1,0:T(8,128)} fusion(f32[8,6,16,256]{3,2,1,0:T(8,128)S(1)} %bitcast.87, s32[1024]{0:T(1024)S(1)} %pad_clamp_fusion.1), kind=kCustom, calls=%fused_computation | custom fusion | bytes 12583168 | tf_op jit(solution)/shard_map/jit(_take)/gather | solution.py:454
  58.8 7.0 %select_select_fusion = f32[64,6,16,256]{3,2,1,0:T(8,128)} fusion(f32[64,6,16,256]{3,2,1,0:T(8,128)} %gather_fusion, pred[64]{0:T(512)(128)(4,1)S(1)} %compare_and_fusion, pred[64]{0:T(512)(128)(4,1)S(1)} %fusion.3), kind=kLoop, calls=%fused_computation.2 | loop fusion | flops 3145728 | bytes 12583040 | tf_op jit(solution)/shard_map/jit(_where)/select_n | solution.py:455
  65.8 9.0 %all-to-all-start.1 = ((f32[64,6,16,256]{3,2,1,0:T(8,128)}), f32[64,6,16,256]{3,2,1,0:T(8,128)}, u32[]{:S(2)}, u32[]{:S(2)}) async-start(f32[64,6,16,256]{3,2,1,0:T(8,128)} %select_select_fusion), calls=%async_computation.1 | async-start | bytes 12582912 | tf_op jit(solution)/shard_map/all_to_all | solution.py:482
  74.9 4.3 %collective-permute-start.2 = (f32[6,1,1,8]{3,0,2,1:T(8,128)S(1)}, f32[6,1,1,8]{3,0,2,1:T(8,128)S(1)}, u32[]{:S(2)}, u32[]{:S(2)}) collective-permute-start(f32[6,1,1,8]{3,0,2,1:T(8,128)S(1)} %bitcast.90), channel_id=1, source_target_pairs={{0,8},{8,16},{16,24},{24,32},{32,40},{40,48},{48,56},{56,64},{64,7... | collective-permute-start | bytes 584 | tf_op jit(solution)/shard_map/ppermute | solution.py:371
  79.4 123.4 %collective-permute-done.2 = f32[6,1,1,8]{3,0,2,1:T(8,128)S(1)} collective-permute-done((f32[6,1,1,8]{3,0,2,1:T(8,128)S(1)}, f32[6,1,1,8]{3,0,2,1:T(8,128)S(1)}, u32[]{:S(2)}, u32[]{:S(2)}) %collective-permute-start.2) | collective-permute-done | bytes 224 | tf_op jit(solution)/shard_map/ppermute | solution.py:371
  202.7 1.9 collective-permute-start.3
  205.0 0.8 collective-permute-done.3
  206.5 20.4 %all-to-all-done.1 = f32[64,6,16,256]{3,2,1,0:T(8,128)} async-done(((f32[64,6,16,256]{3,2,1,0:T(8,128)}), f32[64,6,16,256]{3,2,1,0:T(8,128)}, u32[]{:S(2)}, u32[]{:S(2)}) %all-to-all-start.1) | async-done | bytes 6291488 | tf_op jit(solution)/shard_map/all_to_all | solution.py:482
  226.9 3.4 %gather_fusion.1 = f32[8,6,16,256]{3,2,1,0:T(8,128)S(1)} fusion(f32[64,6,16,256]{3,2,1,0:T(8,128)} %all-to-all-done.1, s32[1024]{0:T(1024)S(1)} %pad_clamp_fusion), kind=kCustom, calls=%fused_computation.1 | custom fusion | bytes 1572896 | tf_op jit(solution)/shard_map/jit(_take)/gather | solution.py:464
  230.3 1.1 broadcast_select_fusion
  (46 shorter events, 7.7 us)
Async XLA Ops:
  1.3 19.6 %collective-permute-start = (f32[3,1,1,8]{3,0,2,1:T(4,128)S(1)}, f32[3,1,1,8]{3,0,2,1:T(4,128)S(1)}, u32[]{:S(2)}, u32[]{:S(2)}) collective-permute-start(f32[3,1,1,8]{3,0,2,1:T(4,128)S(1)} %get-tuple-element.19), channel_id=1, source_target_pairs={{8,0},{16,8},{24,16},{32,24},{40,32},{48,40},{56,48},{64,56},{72,6... | collective-permute-start | bytes 296 | tf_op jit(solution)/shard_map/ppermute | solution.py:371
  11.5 54.3 %all-to-all-start = ((s32[32,2,1]{1,2,0:T(1,128)}), s32[32,2,1]{1,2,0:T(1,128)S(1)}, u32[]{:S(2)}, u32[]{:S(2)}) async-start(s32[32,2,1]{1,2,0:T(1,128)} %bitcast.22), calls=%async_computation | async-start | bytes 32768 | tf_op jit(solution)/shard_map/all_to_all | solution.py:483
  20.9 5.9 %collective-permute-start.1 = (f32[3,2,1,8]{3,0,2,1:T(4,128)S(1)}, f32[3,2,1,8]{3,0,2,1:T(4,128)S(1)}, u32[]{:S(2)}, u32[]{:S(2)}) collective-permute-start(f32[3,2,1,8]{3,0,2,1:T(4,128)S(1)} %constant_dynamic-update-slice_fusion), channel_id=1, source_target_pairs={{1,0},{2,1},{3,2},{4,3},{5,4},{6,5},{7,6},{9,8},{10,9},{11,10},{12... | collective-permute-start | bytes 584 | tf_op jit(solution)/shard_map/ppermute | solution.py:371
  30.7 1.1 copy-start
  31.8 1.1 copy-start.1
  33.0 0.9 copy-start.2
  33.9 0.7 copy-start.3
  34.6 0.7 copy-start.4
  35.3 0.7 copy-start.5
  65.8 161.1 %all-to-all-start.1 = ((f32[64,6,16,256]{3,2,1,0:T(8,128)}), f32[64,6,16,256]{3,2,1,0:T(8,128)}, u32[]{:S(2)}, u32[]{:S(2)}) async-start(f32[64,6,16,256]{3,2,1,0:T(8,128)} %select_select_fusion), calls=%async_computation.1 | async-start | bytes 12582912 | tf_op jit(solution)/shard_map/all_to_all | solution.py:482
  74.9 127.9 %collective-permute-start.2 = (f32[6,1,1,8]{3,0,2,1:T(8,128)S(1)}, f32[6,1,1,8]{3,0,2,1:T(8,128)S(1)}, u32[]{:S(2)}, u32[]{:S(2)}) collective-permute-start(f32[6,1,1,8]{3,0,2,1:T(8,128)S(1)} %bitcast.90), channel_id=1, source_target_pairs={{0,8},{8,16},{16,24},{24,32},{32,40},{40,48},{48,56},{56,64},{64,7... | collective-permute-start | bytes 584 | tf_op jit(solution)/shard_map/ppermute | solution.py:371
  202.7 3.1 %collective-permute-start.3 = (f32[6,2,1,8]{3,0,2,1:T(8,128)S(1)}, f32[6,2,1,8]{3,0,2,1:T(8,128)S(1)}, u32[]{:S(2)}, u32[]{:S(2)}) collective-permute-start(f32[6,2,1,8]{3,0,2,1:T(8,128)S(1)} %pad_maximum_fusion), channel_id=1, source_target_pairs={{0,1},{1,2},{2,3},{3,4},{4,5},{5,6},{6,7},{8,9},{9,10},{10,11},{11... | collective-permute-start | bytes 1160 | tf_op jit(solution)/shard_map/ppermute | solution.py:371

commit v2 on v1

--- a/solution.py
+++ b/solution.py
@@ -1,3 +1,4 @@
+import functools
 import math
 
 import jax
@@ -365,19 +366,257 @@
     return updated, means
 
 
+MESH_ID = pl.DeviceIdType.MESH
+GROUP, COLUMNS, SLOTS, PACK = 32, 8, 8, 2
+
+
+def place(layer, column):
+    return {"rve_0": layer // 4, "rve_1": layer % 4, "mic": column // 2, "mac": column % 2}
+
+
+def own_place():
+    layer = lax.axis_index("rve_0") * 4 + lax.axis_index("rve_1")
+    return layer, lax.axis_index("mic") * 2 + lax.axis_index("mac")
+
+
+def gossip_kernel(
+    row_ref, rows_ref, columns_ref, used_ref, sent, group, second, across, send_a, recv_a, send_b, recv_b
+):
+    layer, column = own_place()
+    barrier = pltpu.get_barrier_semaphore()
+
+    @pl.loop(1, GROUP)
+    def _(step):
+        peer = lax.rem(layer + step, GROUP)
+        pl.semaphore_signal(barrier, inc=1, device_id=place(peer, column), device_id_type=MESH_ID)
+
+    @pl.loop(1, COLUMNS)
+    def _(step):
+        peer = lax.rem(column + step, COLUMNS)
+        pl.semaphore_signal(barrier, inc=1, device_id=place(layer, peer), device_id_type=MESH_ID)
+
+    sent[...] = row_ref[...]
+    group[layer] = row_ref[0]
+    pl.semaphore_wait(barrier, GROUP + COLUMNS - 2)
+
+    def to_layer(step):
+        peer = lax.rem(layer + step, GROUP)
+        return pltpu.make_async_remote_copy(
+            src_ref=sent.at[0],
+            dst_ref=group.at[layer],
+            send_sem=send_a.at[step],
+            recv_sem=recv_a.at[step],
+            device_id=place(peer, column),
+            device_id_type=MESH_ID,
+        )
+
+    def to_column(step):
+        peer = lax.rem(column + step, COLUMNS)
+        return pltpu.make_async_remote_copy(
+            src_ref=second.at[0],
+            dst_ref=across.at[column],
+            send_sem=send_b.at[step],
+            recv_sem=recv_b.at[step],
+            device_id=place(layer, peer),
+            device_id_type=MESH_ID,
+        )
+
+    pl.loop(1, GROUP)(lambda step: to_layer(step).start())
+    pl.loop(1, GROUP)(lambda step: to_layer(step).wait())
+    lane = lax.broadcasted_iota(jnp.int32, (1, 128), 1)
+    used = group[0]
+    for i in range(1, GROUP):
+        used = jnp.maximum(used, group[i])
+    upper = pltpu.roll(group[lax.rem(layer + 1, GROUP)], 32, 1)
+    upper = jnp.where(layer < GROUP - 1, upper, jnp.zeros_like(upper))
+    mixed = jnp.where(lane < 64, used, jnp.where(lane < 96, row_ref[0], upper))
+    second[0] = mixed
+    across[column] = mixed
+    pl.loop(1, COLUMNS)(lambda step: to_column(step).start())
+    pl.loop(1, COLUMNS)(lambda step: to_column(step).wait())
+    used = across[0]
+    for i in range(1, COLUMNS):
+        used = jnp.maximum(used, across[i])
+    used_ref[...] = used
+    rows_ref[...] = group[...]
+    right = across[lax.rem(column + 1, COLUMNS)]
+    columns_ref[0] = across[column]
+    columns_ref[1] = jnp.where(column < COLUMNS - 1, right, jnp.zeros_like(right))
+
+
+def gossip(row):
+    vm = pl.BlockSpec(memory_space=pltpu.VMEM)
+    f32 = jnp.float32
+    return pl.pallas_call(
+        gossip_kernel,
+        out_shape=(
+            jax.ShapeDtypeStruct((GROUP, 1, 128), f32),
+            jax.ShapeDtypeStruct((2, 1, 128), f32),
+            jax.ShapeDtypeStruct((1, 128), f32),
+        ),
+        in_specs=[vm],
+        out_specs=(vm, vm, vm),
+        scratch_shapes=[
+            pltpu.VMEM((1, 1, 128), f32),
+            pltpu.VMEM((GROUP, 1, 128), f32),
+            pltpu.VMEM((1, 1, 128), f32),
+            pltpu.VMEM((COLUMNS, 1, 128), f32),
+            pltpu.SemaphoreType.DMA((GROUP,)),
+            pltpu.SemaphoreType.DMA((GROUP,)),
+            pltpu.SemaphoreType.DMA((COLUMNS,)),
+            pltpu.SemaphoreType.DMA((COLUMNS,)),
+        ],
+        compiler_params=pltpu.CompilerParams(collective_id=0, has_side_effects=True),
+        name="gossip",
+    )(row)
+
+
+def agenda_kernel(here_ref, plan_ref, used_ref, total_ref, shift_ref, pick_ref, land_ref):
+    layer = here_ref[0]
+    total_ref[0] = 0
+
+    @pl.loop(0, GROUP)
+    def _(d):
+        shift_ref[d] = 0
+        pick_ref[d, 0] = 0
+        pick_ref[d, 1] = 0
+        land_ref[d, 0] = SLOTS
+        land_ref[d, 1] = SLOTS
+
+    @pl.loop(0, GROUP)
+    def _(d):
+        @pl.when(used_ref[32 + d] > 0)
+        def _():
+            step = total_ref[0]
+            shift_ref[step] = d
+            total_ref[0] = step + 1
+            target, source = lax.rem(layer + d, GROUP), lax.rem(layer - d + GROUP, GROUP)
+            out_rank, in_rank = jnp.int32(0), jnp.int32(0)
+            for i in range(SLOTS):
+                goes = plan_ref[layer, i] // (SLOTS * COLUMNS) == target
+                value = plan_ref[source, i]
+                comes = value // (SLOTS * COLUMNS) == layer
+
+                @pl.when(goes & (out_rank < PACK))
+                def _():
+                    pick_ref[step, out_rank] = i
+
+                @pl.when(comes & (in_rank < PACK))
+                def _():
+                    land_ref[step, in_rank] = lax.rem(value, SLOTS)
+
+                out_rank = out_rank + goes.astype(jnp.int32)
+                in_rank = in_rank + comes.astype(jnp.int32)
+
+
+def agenda(here, plan, used):
+    sm = pl.BlockSpec(memory_space=pltpu.SMEM)
+    i32 = jnp.int32
+    return pl.pallas_call(
+        agenda_kernel,
+        out_shape=(
+            jax.ShapeDtypeStruct((1,), i32),
+            jax.ShapeDtypeStruct((GROUP,), i32),
+            jax.ShapeDtypeStruct((GROUP, PACK), i32),
+            jax.ShapeDtypeStruct((GROUP, PACK), i32),
+        ),
+        in_specs=[sm] * 3,
+        out_specs=(sm,) * 4,
+        name="agenda",
+    )(here, plan, used)
+
+
+def rotate_kernel(shift, sent_ref, got_ref, arrival, send_sem, recv_sem):
+    layer, column = own_place()
+    target, source = lax.rem(layer + shift, GROUP), lax.rem(layer + GROUP - shift, GROUP)
+    barrier = pltpu.get_barrier_semaphore()
+    pl.semaphore_signal(barrier, inc=1, device_id=place(source, column), device_id_type=MESH_ID)
+    pl.semaphore_wait(barrier, 1)
+    copy = pltpu.make_async_remote_copy(
+        src_ref=sent_ref,
+        dst_ref=arrival,
+        send_sem=send_sem,
+        recv_sem=recv_sem,
+        device_id=place(target, column),
+        device_id_type=MESH_ID,
+    )
+    copy.start()
+    copy.wait()
+    got_ref[...] = arrival[...]
+
+
+def rotate(shift, packets):
+    vm = pl.BlockSpec(memory_space=pltpu.VMEM)
+    return pl.pallas_call(
+        functools.partial(rotate_kernel, shift),
+        out_shape=jax.ShapeDtypeStruct(packets.shape, packets.dtype),
+        in_specs=[vm],
+        out_specs=vm,
+        scratch_shapes=[
+            pltpu.VMEM(packets.shape, packets.dtype),
+            pltpu.SemaphoreType.DMA,
+            pltpu.SemaphoreType.DMA,
+        ],
+        compiler_params=pltpu.CompilerParams(collective_id=shift, has_side_effects=True),
+        name=f"rotate{shift}",
+    )(packets)
+
+
+def land_kernel(step_ref, land_ref, got_ref, held_ref, out_ref, sems):
+    step = step_ref[0]
+    for j in range(PACK):
+        row = land_ref[step, j]
+
+        @pl.when(row < SLOTS)
+        def _():
+            pltpu.make_async_copy(got_ref.at[j], out_ref.at[row], sems.at[j]).start()
+
+    for j in range(PACK):
+        row = land_ref[step, j]
+
+        @pl.when(row < SLOTS)
+        def _():
+            pltpu.make_async_copy(got_ref.at[j], out_ref.at[row], sems.at[j]).wait()
+
+
+def land(step, rows, got, held):
+    vm, sm = pl.BlockSpec(memory_space=pltpu.VMEM), pl.BlockSpec(memory_space=pltpu.SMEM)
+    anywhere = pl.BlockSpec(memory_space=pl.ANY)
+    return pl.pallas_call(
+        land_kernel,
+        out_shape=jax.ShapeDtypeStruct(held.shape, held.dtype),
+        in_specs=[sm, sm, vm, anywhere],
+        out_specs=anywhere,
+        scratch_shapes=[pltpu.SemaphoreType.DMA((PACK,))],
+        input_output_aliases={3: 0},
+        name="land",
+    )(step, rows, got, held)
+
+
+def migrate(updated, total, shifts, picks, rows):
+    branches = [lambda packets: packets] + [functools.partial(rotate, d) for d in range(1, GROUP)]
+
+    def step(state):
+        i, held = state
+        pick = lax.dynamic_slice(picks, (i, 0), (1, PACK))[0]
+        packets = jnp.concatenate(
+            [lax.dynamic_slice(updated, (pick[j], 0, 0), (1, 96, 256)) for j in range(PACK)], axis=0
+        )
+        got = lax.switch(shifts[i], branches, packets)
+        return i + 1, land(i.reshape(1), rows, got, held)
+
+    start = (jnp.int32(0), jnp.zeros_like(updated))
+    return lax.while_loop(lambda state: state[0] < total, step, start)[1]
+
+
 def shifted(value, axis, steps):
     count = lax.axis_size(axis)
     first, last = (max(0, -steps), min(count, count - steps))
     return lax.ppermute(value, axis, [(source, source + steps) for source in range(first, last)])
 
 
-def element_strain(displacement):
-    rows_y = displacement.shape[2]
-    depth = displacement.shape[3]
-    upper_layer = shifted(displacement, RVE, -1)
-    extended = jnp.concatenate([displacement, upper_layer], axis=1)
-    upper_row = shifted(extended, ("mic", "mac"), -1)
-    extended = jnp.concatenate([extended, upper_row], axis=2)
+def element_strain(extended):
+    rows_y, depth = extended.shape[2] - 1, extended.shape[3]
     extended = jnp.pad(extended, ((0, 0), (0, 0), (0, 0), (0, 1)))
     gradient = [[0.0, 0.0, 0.0], [0.0, 0.0, 0.0], [0.0, 0.0, 0.0]]
     for shift_a in (0, 1):
@@ -435,57 +674,32 @@
     return jnp.stack(forces, axis=0)
 
 
-def route_slots(migration_plan, width_rows, capacity):
-    columns = lax.axis_size("mic") * lax.axis_size("mac")
-    target = migration_plan // width_rows
-    partner = target // columns
-    target_row = migration_plan % width_rows
-    shared = partner[:, None] == partner[None, :]
-    positions = jnp.arange(width_rows)
-    earlier = positions[:, None] > positions[None, :]
-    order_within = jnp.sum((shared & earlier).astype(jnp.int32), axis=1)
-    return (partner * capacity + order_within, target_row)
-
-
-def pack_rows(payload, slot_index, total_slots):
-    matches = slot_index[None, :] == jnp.arange(total_slots)[:, None]
-    source = jnp.sum(jnp.where(matches, jnp.arange(payload.shape[0])[None, :], 0), axis=1)
-    filled = jnp.any(matches, axis=1)
-    picked = jnp.take(payload, source, axis=0)
-    return jnp.where(
-        filled.reshape((-1,) + (1,) * (payload.ndim - 1)), picked, jnp.zeros_like(picked)
-    )
-
-
-def unpack_rows(received, labels, width_rows):
-    wanted = labels.astype(jnp.int32) - 1
-    matches = wanted[None, :] == jnp.arange(width_rows)[:, None]
-    source = jnp.sum(jnp.where(matches, jnp.arange(received.shape[0])[None, :], 0), axis=1)
-    return jnp.take(received, source, axis=0)
-
-
 def on_device(
     displacement, plastic, bulk_modulus, shear_modulus, yield_radius, counts, migration_plan
 ):
-    width_rows, depth = plastic.shape[0], displacement.shape[3]
-    strain_rows = element_strain(displacement)
+    depth = displacement.shape[3]
+    layer, column = own_place()
+    shift = (migration_plan // (SLOTS * COLUMNS) - layer + GROUP) % GROUP
+    seen = jnp.any(shift[:, None] == jnp.arange(GROUP)[None, :], axis=0)
+    row = jnp.concatenate(
+        [
+            jnp.pad(migration_plan, (0, 24)).astype(jnp.float32),
+            seen.astype(jnp.float32),
+            jnp.pad(displacement.reshape(3 * depth), (0, 64 - 3 * depth)),
+        ]
+    )
+    rows, columns, used = gossip(row.reshape(1, 1, 128))
+    here = columns[:, 0, 64:].reshape(2, 2, 32)[:, :, : 3 * depth].reshape(2, 2, 3, depth)
+    strain_rows = element_strain(jnp.transpose(here, (2, 1, 0, 3)))
+    total, shifts, picks, landing = agenda(
+        layer.reshape(1), rows[:, 0, :SLOTS].astype(jnp.int32), used[0].astype(jnp.int32)
+    )
     updated, means = solve(
         plastic, strain_rows, counts, bulk_modulus, shear_modulus, yield_radius
     )
-    devices_along = lax.axis_size(RVE)
-    capacity = 2
-    total_slots = devices_along * capacity
-    slot_index, target_row = route_slots(migration_plan, width_rows, capacity)
-    labels = (target_row + 1)[:, None]
-    outgoing = pack_rows(updated.reshape(plastic.shape), slot_index, total_slots)
-    outgoing_labels = pack_rows(labels, slot_index, total_slots)
-    arrived = lax.all_to_all(outgoing, RVE, split_axis=0, concat_axis=0, tiled=True)
-    arrived_labels = lax.all_to_all(
-        outgoing_labels, RVE, split_axis=0, concat_axis=0, tiled=True
-    )
-    plastic_new = unpack_rows(arrived, arrived_labels[:, 0], width_rows)
     force = nodal_forces(means[:, :6], displacement.shape[2], depth)
-    return (force, plastic_new)
+    moved = migrate(updated.reshape(SLOTS, 96, 256), total[0], shifts, picks, landing)
+    return (force, moved.reshape(plastic.shape))
 
 
 def solution(mesh):

time: 232 us -> 155 us (0.67)
  the two profiles are of different devices: /device:TPU:119 before, /device:TPU:24 now
where the time goes in v2:
time: 155 us; the launch traced here: 153 us
  Pallas kernels  104 us (67%)
  loops' own time  21.7 us (14%)
  local copies, waits for them, and re-layouts  15.9 us (10%)
  starting transfers between devices  4.54 us (3%)
  waiting for transfers between devices  2.83 us (2%)
  other arithmetic  2.62 us (2%)
    pallas_call x4, Pallas kernels, rotate(): pl.pallas_call(functools.partial(rotate_kernel, shift), out_shape=jax.Sha...  58.2 us
    another operation x1, loops' own time, migrate(): return lax.while_loop(lambda state: state[0] < total, step, start)[1]  21.4 us
    pallas_call x1, Pallas kernels, solve(): pl.pallas_call(solve_kernel, out_shape=(jax.ShapeDtypeStruct((768, 256),...  19.2 us
    pallas_call x1, Pallas kernels, gossip(): pl.pallas_call(gossip_kernel, out_shape=(jax.ShapeDtypeStruct((GROUP, 1,...  19 us
    unnamed x27, local copies, waits for them, and re-layouts  7.57 us
    ppermute x2, starting transfers between devices, shifted(): lax.ppermute(value, axis, [(source, source + steps) for source in range(f...  4.54 us
    pallas_call x4, Pallas kernels, land(): pl.pallas_call(land_kernel, out_shape=jax.ShapeDtypeStruct(held.shape, he...  4.39 us
    pallas_call x1, Pallas kernels, agenda(): pl.pallas_call(agenda_kernel, out_shape=(jax.ShapeDtypeStruct((1,), i32),...  3.38 us
  transfers between devices with their start and end apart: 2, of which 1 were waited for; matrix products, arithmetic and copies ran while one was open for 6% of the time, Pallas kernels for 43%

profile of v2, /device:TPU:24, one launch (start us, length us, event | category | flops | bytes accessed | tf_op | source)
XLA Modules:
  0.0 152.5 jit_solution(10753819118292467561)
XLA Ops:
  2.7 19.0 %gossip.1 = (f32[32,1,128]{2,1,0:T(1,128)}, f32[2,1,128]{2,1,0:T(1,128)}, f32[1,128]{1,0:T(1,128)}) custom-call(f32[1,1,128]{2,1,0:T(1,128)} %fusion.43.row_ref), custom_call_target="tpu_custom_call" | custom-call | tf_op jit(solution)/shard_map/gossip/pallas_call | solution.py:450
  24.3 1.1 copy-done
  25.5 1.1 copy-done.1
  26.6 0.9 copy-done.2
  27.5 19.2 %solve.1 = (f32[768,256]{1,0:T(8,128)S(1)}, f32[8,128]{1,0:T(8,128)S(1)}) custom-call(f32[768,256]{1,0:T(8,128)S(1)} %bitcast.62, f32[8,6]{1,0:T(8,128)S(1)} %bitcast.63, s32[8,1]{1,0:T(8,128)S(1)} %copy.35.counts_ref, f32[16,256]{1,0:T(8,128)S(1)} %copy-done.3, f32[16,256]{1,0:T(8,128)S(1)} %copy-done.4, f32[16,256]{1,0:T(8,128)S(1)} %copy-done.5, ...), custom_call_target="tpu_custom_call" | custom-call | tf_op jit(solution)/shard_map/solve/pallas_call | solution.py:334
  46.8 2.6 %collective-permute-start = (f32[6,1,1,8]{3,0,1,2:T(8,128)S(1)}, f32[6,1,1,8]{3,0,1,2:T(8,128)S(1)}, u32[]{:S(2)}, u32[]{:S(2)}) collective-permute-start(f32[6,1,1,8]{3,0,1,2:T(8,128)S(1)} %copy.37), channel_id=1, source_target_pairs={{0,8},{8,16},{16,24},{24,32},{32,40},{40,48},{48,56},{56,64},{64,7... | collective-permute-start | bytes 584 | tf_op jit(solution)/shard_map/ppermute | solution.py:615
  51.3 3.4 %agenda.1 = (s32[1]{0:T(128)}, s32[32]{0:T(128)S(1)}, s32[32,2]{1,0:T(8,128)S(1)}, s32[32,2]{1,0:T(8,128)S(1)}) custom-call(s32[1]{0:T(128)} %bitcast.15.here_ref, s32[32,8]{1,0:T(8,128)} %fusion.plan_ref, s32[128]{0:T(128)} %convert_bitcast_fusion.used_ref), custom_call_target="tpu_custom_call" | custom-call | tf_op jit(solution)/shard_map/agenda/pallas_call | solution.py:515
  54.8 92.0 %while.10 = (s32[]{:T(128)}, f32[8,96,256]{2,1,0:T(8,128)S(1)}, s32[]{:T(128)}, s32[32]{0:T(128)S(1)}, s32[32,2]{1,0:T(8,128)S(1)}, /*index=5*/f32[8,96,256]{2,1...) while((s32[]{:T(128)}, f32[8,96,256]{2,1,0:T(8,128)S(1)}, ...), condition=%wide.region_34.35_spmd, body=%wide.region_1.34_spmd.sunk | while | flops 49164 | bytes 1179963 | solution.py:609
  61.2 11.4 %conditional.2 = (f32[2,96,256]{2,1,0:T(8,128)S(1)}) conditional(s32[]{:T(128)} %bitcast.59, f32[2,96,256]{2,1,0:T(8,128)S(1)} %pad_maximum_fusion.4, f32[2,96,256]{2,1,0:T(8,128)S(1)} %pad_maximum_fusion.4, f32[2,96,256]{2,1,0:T(8,128)S(1)} %pad_maximum_fusion.4, f32[2,96,256]{2,1,0:T(8,128)S(1)} %pad_maximum_fusion.4, ...), branch_computations={%region_2.2_spmd, %region_3.3_spmd, %region_4.4_spmd, %region_5.5_... | conditional | bytes 393224 | solution.py:605
  61.2 0.7 copy.116.sent_ref
  61.9 10.6 %rotate1.1 = f32[2,96,256]{2,1,0:T(8,128)S(1)} custom-call(f32[2,96,256]{2,1,0:T(8,128)} %copy.116.sent_ref), custom_call_target="tpu_custom_call" | custom-call | tf_op jit(solution)/shard_map/while/body/cond/branch_1_fun/rotate1/pallas_call | solution.py:550
  72.6 1.1 land.1
  80.1 20.6 %conditional.2 = (f32[2,96,256]{2,1,0:T(8,128)S(1)}) conditional(s32[]{:T(128)} %bitcast.59, f32[2,96,256]{2,1,0:T(8,128)S(1)} %pad_maximum_fusion.4, f32[2,96,256]{2,1,0:T(8,128)S(1)} %pad_maximum_fusion.4, f32[2,96,256]{2,1,0:T(8,128)S(1)} %pad_maximum_fusion.4, f32[2,96,256]{2,1,0:T(8,128)S(1)} %pad_maximum_fusion.4, ...), branch_computations={%region_2.2_spmd, %region_3.3_spmd, %region_4.4_spmd, %region_5.5_... | conditional | bytes 393224 | solution.py:605
  80.2 0.7 copy.125.sent_ref
  80.8 19.8 %rotate10.1 = f32[2,96,256]{2,1,0:T(8,128)S(1)} custom-call(f32[2,96,256]{2,1,0:T(8,128)} %copy.125.sent_ref), custom_call_target="tpu_custom_call" | custom-call | tf_op jit(solution)/shard_map/while/body/cond/branch_10_fun/rotate10/pallas_call | solution.py:550
  100.7 1.1 land.1
  108.2 15.9 %conditional.2 = (f32[2,96,256]{2,1,0:T(8,128)S(1)}) conditional(s32[]{:T(128)} %bitcast.59, f32[2,96,256]{2,1,0:T(8,128)S(1)} %pad_maximum_fusion.4, f32[2,96,256]{2,1,0:T(8,128)S(1)} %pad_maximum_fusion.4, f32[2,96,256]{2,1,0:T(8,128)S(1)} %pad_maximum_fusion.4, f32[2,96,256]{2,1,0:T(8,128)S(1)} %pad_maximum_fusion.4, ...), branch_computations={%region_2.2_spmd, %region_3.3_spmd, %region_4.4_spmd, %region_5.5_... | conditional | bytes 393224 | solution.py:605
  109.0 15.2 %rotate13.1 = f32[2,96,256]{2,1,0:T(8,128)S(1)} custom-call(f32[2,96,256]{2,1,0:T(8,128)} %copy.128.sent_ref), custom_call_target="tpu_custom_call" | custom-call | tf_op jit(solution)/shard_map/while/body/cond/branch_13_fun/rotate13/pallas_call | solution.py:550
  124.1 1.1 land.1
  131.7 13.4 %conditional.2 = (f32[2,96,256]{2,1,0:T(8,128)S(1)}) conditional(s32[]{:T(128)} %bitcast.59, f32[2,96,256]{2,1,0:T(8,128)S(1)} %pad_maximum_fusion.4, f32[2,96,256]{2,1,0:T(8,128)S(1)} %pad_maximum_fusion.4, f32[2,96,256]{2,1,0:T(8,128)S(1)} %pad_maximum_fusion.4, f32[2,96,256]{2,1,0:T(8,128)S(1)} %pad_maximum_fusion.4, ...), branch_computations={%region_2.2_spmd, %region_3.3_spmd, %region_4.4_spmd, %region_5.5_... | conditional | bytes 393224 | solution.py:605
  132.4 12.6 %rotate16.1 = f32[2,96,256]{2,1,0:T(8,128)S(1)} custom-call(f32[2,96,256]{2,1,0:T(8,128)} %copy.131.sent_ref), custom_call_target="tpu_custom_call" | custom-call | tf_op jit(solution)/shard_map/while/body/cond/branch_16_fun/rotate16/pallas_call | solution.py:550
  145.0 1.1 land.1
  146.8 1.9 %collective-permute-start.1 = (f32[6,2,1,8]{3,0,1,2:T(8,128)S(1)}, f32[6,2,1,8]{3,0,1,2:T(8,128)S(1)}, u32[]{:S(2)}, u32[]{:S(2)}) collective-permute-start(f32[6,2,1,8]{3,0,1,2:T(8,128)S(1)} %pad_maximum_fusion.1), channel_id=1, source_target_pairs={{0,1},{1,2},{2,3},{3,4},{4,5},{5,6},{6,7},{8,9},{9,10},{10,11},{11... | collective-permute-start | bytes 1160 | tf_op jit(solution)/shard_map/ppermute | solution.py:615
  148.9 2.8 %collective-permute-done.1 = f32[6,2,1,8]{3,0,1,2:T(8,128)S(1)} collective-permute-done((f32[6,2,1,8]{3,0,1,2:T(8,128)S(1)}, f32[6,2,1,8]{3,0,1,2:T(8,128)S(1)}, u32[]{:S(2)}, u32[]{:S(2)}) %collective-permute-start.1) | collective-permute-done | bytes 416 | tf_op jit(solution)/shard_map/ppermute | solution.py:615
  (75 shorter events, 13.9 us)
Async XLA Ops:
  0.6 0.7 copy-start.11
  1.3 0.7 copy-start.8
  21.7 0.6 copy-start.9
  22.8 1.0 copy-start.5
  22.9 0.7 copy-start.10
  23.6 0.7 copy-start.3
  23.6 0.7 copy-start.4
  24.3 1.1 copy-start
  25.5 1.1 copy-start.1
  26.6 0.9 copy-start.2
  46.7 2.7 %copy-start.7 = (f32[32,1,128]{2,1,0:T(1,128)S(1)}, f32[32,1,128]{2,1,0:T(1,128)}, u32[]{:S(2)}) copy-start(f32[32,1,128]{2,1,0:T(1,128)} %get-tuple-element.116) | copy-start | bytes 49156
  46.8 99.9 %collective-permute-start = (f32[6,1,1,8]{3,0,1,2:T(8,128)S(1)}, f32[6,1,1,8]{3,0,1,2:T(8,128)S(1)}, u32[]{:S(2)}, u32[]{:S(2)}) collective-permute-start(f32[6,1,1,8]{3,0,1,2:T(8,128)S(1)} %copy.37), channel_id=1, source_target_pairs={{0,8},{8,16},{16,24},{24,32},{32,40},{40,48},{48,56},{56,64},{64,7... | collective-permute-start | bytes 584 | tf_op jit(solution)/shard_map/ppermute | solution.py:615
  50.1 0.7 copy-start.12
  146.8 5.8 %copy-start.6 = (f32[8,96,256]{2,1,0:T(8,128)}, f32[8,96,256]{2,1,0:T(8,128)S(1)}, u32[]{:S(2)}) copy-start(f32[8,96,256]{2,1,0:T(8,128)S(1)} %get-tuple-element.123) | copy-start | bytes 2359300
  146.8 5.0 %collective-permute-start.1 = (f32[6,2,1,8]{3,0,1,2:T(8,128)S(1)}, f32[6,2,1,8]{3,0,1,2:T(8,128)S(1)}, u32[]{:S(2)}, u32[]{:S(2)}) collective-permute-start(f32[6,2,1,8]{3,0,1,2:T(8,128)S(1)} %pad_maximum_fusion.1), channel_id=1, source_target_pairs={{0,1},{1,2},{2,3},{3,4},{4,5},{5,6},{6,7},{8,9},{9,10},{10,11},{11... | collective-permute-start | bytes 1160 | tf_op jit(solution)/shard_map/ppermute | solution.py:615
